TPU v7x, 256 devices: a whole 4x4x8 slice. The times are simulated.
256 devices in a mesh: row: 32 (over y, x, core), col: 8 (over z).
Axes of the slice: x: 4, y: 4, z: 8, core: 2. Of those that a mesh axis runs over, the one named last changes fastest.
Arguments:
- hidden: bfloat16 [2048, 2560], P(None, 'row'), may hold values from -6 to 6
- w_qkv: bfloat16 [2560, 3584], P('row', 'col'), may hold values from -8 to 8
- page_table: int32 [64, 64], P('row'), may hold values from -1 to 127, as said below
- prompt_lengths: int32 [64], P('row'), may hold values from 1 to 8192, as said below
- page_keys: bfloat16 [32, 128, 128, 512], P('row', 'col'), may hold values from -4 to 4
- page_values: bfloat16 [32, 128, 128, 512], P('row', 'col'), may hold values from -6 to 6
- tail_lengths: int32 [64, 16], P('row'), may hold values from 0 to 512
- tail_keys: bfloat16 [64, 16, 512, 512], P('row', 'col'), may hold values from -6 to 6
- tail_values: bfloat16 [64, 16, 512, 512], P('row', 'col'), may hold values from -6 to 6
Outputs:
- attended: bfloat16 [64, 16, 2, 2560], P('row', 'col')
Inputs may be any that keep to these rules, and one draw needn't show every extreme that they name: `page_table`: entry j of prompt p is the slot of block p // 2 that holds its tokens j * 128 to (j + 1) * 128 - 1 where j * 128 < prompt_lengths[p], else -1; the live slots of a block are distinct. Slot k of a block lies on the device of col index k // 16. The live pages of a block fill the devices' slots one device after another, in an order drawn from the seed, so that at least one device holds 16 live pages. `prompt_lengths`: every block of 2 prompts holds a prompt of 8192 tokens.
All inputs are finite; a program needn't handle non-finite values.
Results may differ from a plain program's by a relative error of at most 0.015.
The roundings to bfloat16 on the way count: a program that leaves them out, or rounds other values in their place, can miss the bound.
Values may be sent and summed in bfloat16 or wider, within the bound.
A program may use at most 64 MiB of HBM per device.

v0:
```python
import math
import jax
import jax.numpy as jnp
from jax import lax
from jax.sharding import PartitionSpec as P

HEADS = 20
KVH = 4
HD = 128
SAMPLES = 16
rope_base = 500000.0
masked_score = -1e30


def merged(value, axis, join):
    pieces = jax.tree.map(lambda part: lax.all_gather(part, axis), value)
    head = jax.tree.map(lambda part: part[0], pieces)
    tail = jax.tree.map(lambda part: part[1:], pieces)
    total, _ = lax.scan(lambda total, section: (join(total, section), None), head, tail)
    return total


def rotate(vectors, positions):
    half_size = vectors.shape[-1] // 2
    frequency = jnp.exp(
        jnp.arange(half_size, dtype=jnp.float32) * (-2.0 * math.log(rope_base) / vectors.shape[-1])
    )
    angles = positions.astype(jnp.float32)[..., None, None] * frequency
    cosine = jnp.cos(angles)
    sines = jnp.sin(angles)
    leading = vectors[..., :half_size].astype(jnp.float32)
    trailing = vectors[..., half_size:].astype(jnp.float32)
    return jnp.concatenate(
        [leading * cosine - trailing * sines, trailing * cosine + leading * sines], axis=-1
    )


def combine_states(earlier, later):
    top_early, sums_early, acc_early = earlier
    top_late, sums_late, acc_late = later
    highest = jnp.maximum(top_early, top_late)
    scale_early = jnp.exp(top_early - highest)
    scale_late = jnp.exp(top_late - highest)
    return (
        highest,
        sums_early * scale_early + sums_late * scale_late,
        acc_early * scale_early[..., None] + acc_late * scale_late[..., None],
    )


def project_rows(hidden, weights):
    return jnp.dot(hidden, weights, preferred_element_type=jnp.float32)


def local(
    hidden,
    w_qkv,
    page_table,
    prompt_lengths,
    page_keys,
    page_values,
    tail_lengths,
    tail_keys,
    tail_values,
):
    group_size = HEADS // KVH
    q_width = HEADS * HD
    kv_width = KVH * HD
    score_scale = 1.0 / math.sqrt(HD)
    column_sums = lax.psum_scatter(
        project_rows(hidden, w_qkv), "row", scatter_dimension=0, tiled=True
    ).astype(jnp.bfloat16)
    projected = lax.all_gather(column_sums, "col", axis=1, tiled=True)
    prompts_here = prompt_lengths.shape[0]
    projected = projected.reshape(prompts_here, SAMPLES, 2, projected.shape[-1])
    steps_ahead = jnp.arange(2, dtype=jnp.int32)
    positions = (
        prompt_lengths[:, None, None] + tail_lengths[:, :, None] + steps_ahead[None, None, :]
    )
    queries = rotate(
        projected[..., :q_width].reshape(prompts_here, SAMPLES, 2, HEADS, HD), positions
    ).astype(jnp.bfloat16)
    new_keys = rotate(
        projected[..., q_width : q_width + kv_width].reshape(prompts_here, SAMPLES, 2, KVH, HD),
        positions,
    ).astype(jnp.bfloat16)
    new_values = projected[..., q_width + kv_width :].reshape(prompts_here, SAMPLES, 2, KVH, HD)
    pool_keys = page_keys[0]
    pool_values = page_values[0]
    pool_slots = pool_keys.shape[0]
    page_size = pool_keys.shape[1]
    slot_ids = lax.axis_index("col") * pool_slots + jnp.arange(pool_slots, dtype=jnp.int32)
    matches = (page_table[None, :, :] == slot_ids[:, None, None]).astype(jnp.int32)
    owners = jnp.sum(matches, axis=2)
    page_index = jnp.sum(
        matches * jnp.arange(page_table.shape[1], dtype=jnp.int32)[None, None, :], axis=(1, 2)
    )
    slot_prompt = jnp.sum(owners * jnp.arange(prompts_here, dtype=jnp.int32)[None, :], axis=1)
    slot_length = jnp.sum(owners * prompt_lengths[None, :], axis=1)
    key_positions = (
        page_index[:, None] * page_size + jnp.arange(page_size, dtype=jnp.int32)[None, :]
    )
    visible = (key_positions < slot_length[:, None])[:, None, None, None, :]
    query_grid = queries.reshape(prompts_here, SAMPLES * 2, KVH, group_size, HD)
    slot_queries = jnp.take(query_grid, slot_prompt, axis=0)
    page_scores = (
        jnp.einsum(
            "sqkgd,spkd->sqkgp",
            slot_queries,
            pool_keys.reshape(pool_slots, page_size, KVH, HD),
            preferred_element_type=jnp.float32,
        )
        * score_scale
    )
    page_scores = jnp.where(visible, page_scores, masked_score)
    slot_top = jnp.max(page_scores, axis=-1)
    prompt_top = jnp.max(
        jnp.where(owners[:, :, None, None, None] > 0, slot_top[:, None], masked_score), axis=0
    )
    slot_shift = jnp.take(prompt_top, slot_prompt, axis=0)
    page_weights = jnp.where(visible, jnp.exp(page_scores - slot_shift[..., None]), 0.0)
    slot_sums = jnp.sum(page_weights, axis=-1)
    slot_acc = jnp.einsum(
        "sqkgp,spkd->sqkgd",
        page_weights.astype(jnp.bfloat16),
        pool_values.reshape(pool_slots, page_size, KVH, HD),
        preferred_element_type=jnp.float32,
    )
    owner_float = owners.astype(jnp.float32)
    prefix_sums = jnp.einsum(
        "sr,sqkg->rqkg", owner_float, slot_sums, precision=lax.Precision.HIGHEST
    )
    prefix_acc = jnp.einsum(
        "sr,sqkgd->rqkgd", owner_float, slot_acc, precision=lax.Precision.HIGHEST
    )
    state_shape = (prompts_here, SAMPLES, 2, KVH, group_size)
    prefix_top = prompt_top.reshape(state_shape)
    prefix_sums = prefix_sums.reshape(state_shape)
    prefix_acc = prefix_acc.reshape(state_shape + (HD,))
    own_count = tail_keys.shape[1]
    own_start = lax.axis_index("col") * own_count
    whole_top, whole_sums, whole_acc = merged(
        (prefix_top, prefix_sums, prefix_acc), "col", combine_states
    )
    merged_top = lax.dynamic_slice_in_dim(whole_top, own_start, own_count, 1)
    merged_sums = lax.dynamic_slice_in_dim(whole_sums, own_start, own_count, 1)
    merged_acc = lax.dynamic_slice_in_dim(whole_acc, own_start, own_count, 1)
    own_queries = lax.dynamic_slice_in_dim(queries, own_start, own_count, 1).reshape(
        prompts_here, own_count, 2, KVH, group_size, HD
    )
    own_keys = lax.dynamic_slice_in_dim(new_keys, own_start, own_count, 1)
    own_values = lax.dynamic_slice_in_dim(new_values, own_start, own_count, 1)
    own_tails = lax.dynamic_slice_in_dim(tail_lengths, own_start, own_count, 1)
    tail_room = tail_keys.shape[2]
    tail_grid = tail_keys.reshape(prompts_here, own_count, tail_room, KVH, HD)
    tail_scores = (
        jnp.einsum(
            "rstkgd,rsjkd->rstkgj", own_queries, tail_grid, preferred_element_type=jnp.float32
        )
        * score_scale
    )
    tail_seen = (jnp.arange(tail_room, dtype=jnp.int32)[None, None, :] < own_tails[:, :, None])[
        :, :, None, None, None, :
    ]
    tail_scores = jnp.where(tail_seen, tail_scores, masked_score)
    fresh_scores = (
        jnp.einsum(
            "rstkgd,rsukd->rstkgu", own_queries, own_keys, preferred_element_type=jnp.float32
        )
        * score_scale
    )
    causal = (steps_ahead[None, :] <= steps_ahead[:, None])[None, None, :, None, None, :]
    fresh_scores = jnp.where(causal, fresh_scores, masked_score)
    local_top = jnp.maximum(jnp.max(tail_scores, axis=-1), jnp.max(fresh_scores, axis=-1))
    tail_weights = jnp.where(tail_seen, jnp.exp(tail_scores - local_top[..., None]), 0.0)
    fresh_weights = jnp.where(causal, jnp.exp(fresh_scores - local_top[..., None]), 0.0)
    local_sums = jnp.sum(tail_weights, axis=-1) + jnp.sum(fresh_weights, axis=-1)
    local_acc = jnp.einsum(
        "rstkgj,rsjkd->rstkgd",
        tail_weights.astype(jnp.bfloat16),
        tail_values.reshape(prompts_here, own_count, tail_room, KVH, HD),
        preferred_element_type=jnp.float32,
    )
    local_acc = local_acc + jnp.einsum(
        "rstkgu,rsukd->rstkgd",
        fresh_weights.astype(jnp.bfloat16),
        own_values,
        preferred_element_type=jnp.float32,
    )
    final_top, final_sums, final_acc = combine_states(
        (merged_top, merged_sums, merged_acc), (local_top, local_sums, local_acc)
    )
    attended = final_acc / final_sums[..., None]
    return attended.reshape(prompts_here, own_count, 2, HEADS * HD).astype(jnp.bfloat16)


def solution(mesh):
    in_specs = (
        P(None, "row"),
        P("row", "col"),
        P("row", None),
        P("row"),
        P("row", "col", None, None),
        P("row", "col", None, None),
        P("row", None),
        P("row", "col", None, None),
        P("row", "col", None, None),
    )
    out_specs = P("row", "col", None, None)
    return jax.shard_map(local, mesh=mesh, in_specs=in_specs, out_specs=out_specs, check_vma=False)
```

profile of v0, /device:TPU:6, one launch (start us, length us, event | category | flops | bytes accessed | tf_op | source)
XLA Modules:
  0.0 266.6 jit_solution(7269477015864981519)
XLA Ops:
  7.5 3.6 %fusion.110 = f32[2048,448]{1,0:T(8,128)} fusion(bf16[2048,80]{0,1:T(8,128)(2,1)S(1)} %copy-done, bf16[80,448]{1,0:T(8,128)(2,1)} %param.12), kind=kOutput, calls=%fused_computation.142 | convolution fusion | flops 146800640 | bytes 4069376 | tf_op jit(solution)/shard_map/dot_general | solution.py:52
  11.2 2.1 reshape_squeeze.6
  13.3 4.0 %reshape_squeeze.7 = bf16[16,128,4,128]{3,2,1,0:T(4,128)(2,1)} reshape(bf16[1,16,128,512]{3,2,1,0:T(8,128)(2,1)} %param.16) | data formatting | bytes 4194304 | tf_op jit(solution)/shard_map/reshape;squeeze | solution.py:126
  18.0 85.4 %reduce-scatter.2.cloned.1.call-done = f32[64,448]{1,0:T(8,128)} async-done(((f32[2048,448]{1,0:T(8,128)}), f32[64,448]{1,0:T(8,128)}) %reduce-scatter.2.cloned.1.call-update) | async-done | bytes 114704 | tf_op jit(solution)/shard_map/reduce_scatter | solution.py:70
  104.4 26.7 %all-gather.1 = bf16[8,448,64]{1,2,0:T(8,128)(2,1)S(1)} all-gather(bf16[1,448,64]{1,2,0:T(8,128)(2,1)S(1)} %convert_bitcast_fusion), channel_id=1, replica_groups=mesh['row'=32,'col'=8] {'col'}, dimensions={0}, use_global_device_ids=true | all-gather | bytes 516096 | tf_op jit(solution)/shard_map/all_gather | solution.py:73
  136.1 5.7 %bitcast_reduce_fusion = (f32[16,32,4,5]{1,3,2,0:T(8,128)S(1)}, f32[16,4,32,5,128]{4,2,3,1,0:T(8,128)}) fusion(pred[16,128]{1,0:T(8,128)(4,1)S(1)} %add_compare_fusion, bf16[16,128,4,128,1]{3,2,1,0,4:T(4,128)(2,1)} %bitcast.114, bf16[16,32,4,5,128]{4,1,3,2,0:T(8,128)(2,1)S(1)} %gather_fusion, pred[16]{0:T(512)(128)(4,1)S(1)} %compare_and_fusion), kind=kOutput, calls=%fused_computation.13 | convolution fusion | flops 340776960 | bytes 10004496 | tf_op jit(solution)/shard_map/sqkgd,spkd->sqkgp/dot_general | solution.py:107
  142.8 4.2 %fusion.21 = f32[16,32,4,5,128]{4,1,3,2,0:T(8,128)S(1)} fusion(f32[16,4,32,5,128]{4,2,3,1,0:T(8,128)} %get-tuple-element.131, f32[16,32,4,5]{1,3,2,0:T(8,128)S(1)} %copy.180, pred[16,128]{1,0:T(8,128)(4,1)S(1)} %add_compare_fusion, bf16[16,128,4,128,1]{3,2,1,0,4:T(4,128)(2,1)} %bitcast.113), kind=kOutput, calls=%fused_computation.31 | convolution fusion | flops 342097920 | bytes 12625920 | tf_op jit(solution)/shard_map/sqkgp,spkd->sqkgd/dot_general | solution.py:123
  147.0 7.4 %fusion.6 = f32[2,32,4,5,128]{4,0,3,2,1:T(2,128)S(1)} fusion(f32[16,32,4,5,128]{4,1,3,2,0:T(8,128)S(1)} %fusion.21, s32[16,2]{0,1:T(2,128)S(1)} %get-tuple-element.90), kind=kOutput, calls=%fused_computation.16 | convolution fusion | flops 31457312 | bytes 5898368 | tf_op jit(solution)/shard_map/sr,sqkgd->rqkgd/dot_general | solution.py:133
  155.5 2.6 reshape.151
  158.0 4.0 %reshape.153 = bf16[2,2,512,4,128]{4,3,2,1,0:T(4,128)(2,1)} reshape(bf16[2,2,512,512]{3,2,1,0:T(8,128)(2,1)} %param.19) | data formatting | bytes 4194304 | tf_op jit(solution)/shard_map/reshape | solution.py:181
  163.0 5.9 %fusion.9 = f32[16,32,4,5]{1,3,2,0:T(8,128)} fusion(f32[16,4,32,5,128]{4,2,3,1,0:T(8,128)} %get-tuple-element.131, f32[16,32,4,5]{1,3,2,0:T(8,128)S(1)} %copy.180, pred[16,128]{1,0:T(8,128)(4,1)S(1)} %add_compare_fusion), kind=kLoop, calls=%fused_computation.20 | loop fusion | flops 6543360 | bytes 5326848 | tf_op jit(solution)/shard_map/reduce_sum | solution.py:122
  170.0 2.4 fusion.66
  172.4 26.0 %all-gather = f32[16,16,2,4,5]{1,3,4,2,0:T(4,128)S(1)} all-gather(f32[2,16,2,4,5]{1,3,4,2,0:T(4,128)S(1)} %copy.183), channel_id=2, replica_groups=mesh['row'=32,'col'=8] {'col'}, dimensions={0}, use_global_device_ids=true | all-gather | bytes 46080 | tf_op jit(solution)/shard_map/all_gather | solution.py:16
  198.4 1.6 fusion.105
  200.0 1.5 reshape.185
  202.7 26.0 %all_gather.13 = f32[8,2,16,2,4,5]{2,4,5,3,1,0:T(4,128)S(1)} all-gather(f32[1,2,16,2,4,5]{2,4,5,3,1,0:T(4,128)S(1)} %copy.178), channel_id=1, replica_groups=mesh['row'=32,'col'=8] {'col'}, dimensions={0}, use_global_device_ids=true | all-gather | bytes 46080 | tf_op jit(solution)/shard_map/all_gather | solution.py:16
  234.8 5.0 %slice.66 = f32[7,2,16,2,4,5,128]{6,2,5,4,3,1,0:T(8,128)} slice(f32[8,2,16,2,4,5,128]{6,2,5,4,3,1,0:T(8,128)} %all-gather.4.cloned.1.call-done), slice={[1:8], [0:2], [0:16], [0:2], [0:4], [0:5], [0:128]} | slice | bytes 9175040 | tf_op jit(solution)/shard_map/slice | solution.py:18
  239.8 16.7 %while.14 = (s32[]{:T(128)}, f32[2,16,2,4,5]{1,3,4,2,0:T(4,128)S(1)}, f32[2,16,2,4,5]{1,3,4,2,0:T(4,128)S(1)}, f32[2,16,2,4,5,128]{5,4,3,2,1,0:T(8,128)S(1)}, f3...) while((s32[]{:T(128)}, ...), condition=%wide.region_9.10_spmd, body=%wide.region_8.9_spmd.sunk | while | flops 499202 | bytes 3348581 | solution.py:19
  240.2 1.1 constant_dynamic-slice_fusion.3
  242.6 1.1 constant_dynamic-slice_fusion.3
  245.0 1.1 constant_dynamic-slice_fusion.3
  247.4 1.1 constant_dynamic-slice_fusion.3
  249.8 1.1 constant_dynamic-slice_fusion.3
  256.9 2.1 fusion.55
  (123 shorter events, 30.9 us)
Async XLA Ops:
  6.5 1.0 copy-start
  6.5 4.6 %copy-start.5 = (bf16[1,16,128,512]{3,2,1,0:T(8,128)(2,1)S(1)}, bf16[1,16,128,512]{3,2,1,0:T(8,128)(2,1)}, u32[]{:S(2)}) copy-start(bf16[1,16,128,512]{3,2,1,0:T(8,128)(2,1)} %param.15) | copy-start | bytes 6291460
  6.5 96.9 %reduce-scatter.2.cloned.1.call-start = ((), (), s32[]{:S(2)}) async-start(), calls=%async_computation.1 | async-start | bytes 4325376 | tf_op jit(solution)/shard_map/reduce_scatter | solution.py:70
  11.1 222.2 %all-gather.4.cloned.1.call-start = ((), (), s32[]{:S(2)}) async-start(), calls=%async_computation.2 | async-start | bytes 5898240 | tf_op jit(solution)/shard_map/all_gather | solution.py:16
  11.2 6.1 %copy-start.12 = (s32[2,64]{1,0:T(2,128)S(1)}, s32[2,64]{1,0:T(2,128)}, u32[]{:S(2)}) copy-start(s32[2,64]{1,0:T(2,128)} %param.13) | copy-start | bytes 1540
  11.2 6.3 %copy-start.11 = (s32[2]{0:T(128)S(1)}, s32[2]{0:T(128)}, u32[]{:S(2)}) copy-start(s32[2]{0:T(128)} %param.14) | copy-start | bytes 28
  11.2 6.4 %copy-start.10 = (s32[2,16]{1,0:T(2,128)S(1)}, s32[2,16]{1,0:T(2,128)}, u32[]{:S(2)}) copy-start(s32[2,16]{1,0:T(2,128)} %param.17) | copy-start | bytes 388
  18.0 116.2 %copy-start.8 = (f32[2,16,2,64]{3,1,2,0:T(8,128)}, f32[2,16,2,64]{3,1,2,0:T(8,128)S(1)}, u32[]{:S(2)}) copy-start(f32[2,16,2,64]{3,1,2,0:T(8,128)S(1)} %get-tuple-element.124) | copy-start | bytes 49156
  18.0 116.2 %copy-start.9 = (f32[2,16,2,64]{3,1,2,0:T(8,128)}, f32[2,16,2,64]{3,1,2,0:T(8,128)S(1)}, u32[]{:S(2)}) copy-start(f32[2,16,2,64]{3,1,2,0:T(8,128)S(1)} %get-tuple-element.125) | copy-start | bytes 49156
  132.1 0.8 copy-start.6
  133.9 0.8 copy-start.1
  133.9 1.0 copy-start.3
  162.2 39.3 %copy-start.2 = (bf16[2,16,2,20,64]{4,3,1,2,0:T(8,128)(2,1)S(1)}, bf16[2,16,2,20,64]{4,3,1,2,0:T(8,128)(2,1)}, u32[]{:S(2)}) copy-start(bf16[2,16,2,20,64]{4,3,1,2,0:T(8,128)(2,1)} %copy-done.1) | copy-start | bytes 491524
  162.2 39.3 %copy-start.4 = (bf16[2,16,2,20,64]{4,3,1,2,0:T(8,128)(2,1)S(1)}, bf16[2,16,2,20,64]{4,3,1,2,0:T(8,128)(2,1)}, u32[]{:S(2)}) copy-start(bf16[2,16,2,20,64]{4,3,1,2,0:T(8,128)(2,1)} %copy-done.3) | copy-start | bytes 491524
  228.7 3.6 %copy-start.7 = (f32[8,2,16,2,4,5]{2,4,5,3,1,0:T(4,128)}, f32[8,2,16,2,4,5]{2,4,5,3,1,0:T(4,128)S(1)}, u32[]{:S(2)}) copy-start(f32[8,2,16,2,4,5]{2,4,5,3,1,0:T(4,128)S(1)} %all_gather.13) | copy-start | bytes 122884
  234.7 5.0 %slice-start = ((f32[8,2,16,2,4,5]{2,4,5,3,1,0:T(4,128)}), f32[7,2,16,2,4,5]{2,4,5,3,1,0:T(4,128)S(1)}, s32[]{:S(2)}) async-start(f32[8,2,16,2,4,5]{2,4,5,3,1,0:T(4,128)} %copy-done.7), calls=%async_computation.3 | async-start | bytes 573440 | tf_op jit(solution)/shard_map/slice | solution.py:18
Sparse Core Ops, SparseCore 0:
  11.3 92.0 reduce-scatter.1
  155.6 68.7 all-gather.3
where the time goes:
time: 268 us; the launch traced here: 267 us
  waiting for transfers between devices  85.4 us (32%)
  blocking collectives  78.7 us (29%)
  local copies, waits for them, and re-layouts  45.2 us (17%)
  matrix products  27.5 us (10%)
  other arithmetic  15.7 us (6%)
  between operations  13.8 us (5%)
    reduce_scatter x1, waiting for transfers between devices, local(): lax.psum_scatter(project_rows(hidden, w_qkv), 'row', scatter_dimension=0,...  85.4 us
    all_gather x2, blocking collectives, merged(): pieces = jax.tree.map(lambda part: lax.all_gather(part, axis), value)  51.9 us
    all_gather x1, blocking collectives, local(): projected = lax.all_gather(column_sums, 'col', axis=1, tiled=True)  26.7 us
    dynamic_slice x7, local copies, waits for them, and re-layouts, merged(): lax.scan(lambda total, section: (join(total, section), None), head, tail)  7.99 us
    dot_general x1, matrix products, local(): jnp.einsum('sr,sqkgd->rqkgd', owner_float, slot_acc, precision=lax.Precis...  7.38 us
    reduce_sum x1, other arithmetic, local(): slot_sums = jnp.sum(page_weights, axis=-1)  5.86 us
    dot_general x1, matrix products, local(): jnp.einsum('sqkgd,spkd->sqkgp', slot_queries, pool_keys.reshape(pool_slot...  5.66 us
    add x7, other arithmetic, combine_states(): acc_early * scale_early[..., None] + acc_late * scale_late[..., None]  5.49 us
  transfers between devices with their start and end apart: 2, of which 1 were waited for; matrix products, arithmetic and copies ran while one was open for 12% of the time, Pallas kernels for 0%

commit v1 on v0

--- a/solution.py
+++ b/solution.py
@@ -70,7 +70,13 @@
     column_sums = lax.psum_scatter(
         project_rows(hidden, w_qkv), "row", scatter_dimension=0, tiled=True
     ).astype(jnp.bfloat16)
-    projected = lax.all_gather(column_sums, "col", axis=1, tiled=True)
+    size = lax.axis_size("col")
+    current, blocks = (column_sums, [column_sums])
+    for _ in range(size - 1):
+        current = lax.ppermute(current, "col", [(i, (i + 1) % size) for i in range(size)])
+        blocks.insert(0, current)
+    line = jnp.concatenate(blocks, axis=1)
+    projected = jnp.roll(line, (lax.axis_index("col") + 1) * column_sums.shape[1], axis=1)
     prompts_here = prompt_lengths.shape[0]
     projected = projected.reshape(prompts_here, SAMPLES, 2, projected.shape[-1])
     steps_ahead = jnp.arange(2, dtype=jnp.int32)

time: 268 us -> 282 us (1.052)
  waiting for transfers between devices: 85.4 us -> 123 us
  blocking collectives: 78.7 us -> 52.7 us
    ppermute x0 -> x7, waiting for transfers between devices: none -> 30.9 us  [local(): lax.ppermute(current, 'col', [(i, (i + 1) % size) for i in range(size)])]
    all_gather x1 -> x0, blocking collectives: 26.7 us -> none  [local(): projected = lax.all_gather(column_sums, 'col', axis=1, tiled=True)]
    reduce_scatter x1, waiting for transfers between devices: 85.4 us -> 91.7 us  [local(): lax.psum_scatter(project_rows(hidden, w_qkv), 'row', scatter_dimension=0,...]
  transfers between devices with their start and end apart: 2 -> 9, of which waited for: 1 -> 7; matrix products, arithmetic and copies ran while one was open for 12% -> 12% of each run, Pallas kernels for 0% -> 0%
where the time goes in v1:
time: 282 us; the launch traced here: 280 us
  waiting for transfers between devices  123 us (44%)
  blocking collectives  52.7 us (19%)
  local copies, waits for them, and re-layouts  44.9 us (16%)
  matrix products  27.4 us (10%)
  other arithmetic  15.8 us (6%)
  between operations  13.8 us (5%)
    reduce_scatter x1, waiting for transfers between devices, local(): lax.psum_scatter(project_rows(hidden, w_qkv), 'row', scatter_dimension=0,...  91.7 us
    all_gather x2, blocking collectives, merged(): pieces = jax.tree.map(lambda part: lax.all_gather(part, axis), value)  52.7 us
    ppermute x7, waiting for transfers between devices, local(): lax.ppermute(current, 'col', [(i, (i + 1) % size) for i in range(size)])  30.9 us
    dynamic_slice x7, local copies, waits for them, and re-layouts, merged(): lax.scan(lambda total, section: (join(total, section), None), head, tail)  7.99 us
    dot_general x1, matrix products, local(): jnp.einsum('sr,sqkgd->rqkgd', owner_float, slot_acc, precision=lax.Precis...  7.38 us
    reduce_sum x1, other arithmetic, local(): slot_sums = jnp.sum(page_weights, axis=-1)  5.95 us
  transfers between devices with their start and end apart: 9, of which 7 were waited for; matrix products, arithmetic and copies ran while one was open for 12% of the time, Pallas kernels for 0%

profile of v1, /device:TPU:6, one launch (start us, length us, event | category | flops | bytes accessed | tf_op | source)
XLA Modules:
  0.0 280.3 jit_solution(1527132033127091374)
XLA Ops:
  7.5 3.6 %fusion.110 = f32[2048,448]{1,0:T(8,128)} fusion(bf16[2048,80]{0,1:T(8,128)(2,1)S(1)} %copy-done, bf16[80,448]{1,0:T(8,128)(2,1)} %param.12), kind=kOutput, calls=%fused_computation.142 | convolution fusion | flops 146800640 | bytes 4069376 | tf_op jit(solution)/shard_map/dot_general | solution.py:52
  11.7 91.7 %reduce-scatter.2.cloned.1.call-done = f32[64,448]{1,0:T(8,128)} async-done(((f32[2048,448]{1,0:T(8,128)}), f32[64,448]{1,0:T(8,128)}) %reduce-scatter.2.cloned.1.call-update) | async-done | bytes 114704 | tf_op jit(solution)/shard_map/reduce_scatter | solution.py:70
  104.4 1.6 collective-permute-start
  106.0 4.0 %collective-permute-done = bf16[64,448]{1,0:T(8,128)(2,1)S(1)} collective-permute-done((bf16[64,448]{1,0:T(8,128)(2,1)S(1)}, bf16[64,448]{1,0:T(8,128)(2,1)S(1)}, u32[]{:S(2)}, u32[]{:S(2)}) %collective-permute-start) | collective-permute-done | bytes 57376 | tf_op jit(solution)/shard_map/ppermute | solution.py:76
  111.0 5.1 %collective-permute-done.1 = bf16[64,448]{1,0:T(8,128)(2,1)S(1)} collective-permute-done((bf16[64,448]{1,0:T(8,128)(2,1)S(1)}, bf16[64,448]{1,0:T(8,128)(2,1)S(1)}, u32[]{:S(2)}, u32[]{:S(2)}) %collective-permute-start.1) | collective-permute-done | bytes 57376 | tf_op jit(solution)/shard_map/ppermute | solution.py:76
  116.2 5.4 %collective-permute-done.2 = bf16[64,448]{1,0:T(8,128)(2,1)S(1)} collective-permute-done((bf16[64,448]{1,0:T(8,128)(2,1)S(1)}, bf16[64,448]{1,0:T(8,128)(2,1)S(1)}, u32[]{:S(2)}, u32[]{:S(2)}) %collective-permute-start.2) | collective-permute-done | bytes 57376 | tf_op jit(solution)/shard_map/ppermute | solution.py:76
  121.6 5.5 %collective-permute-done.3 = bf16[64,448]{1,0:T(8,128)(2,1)S(1)} collective-permute-done((bf16[64,448]{1,0:T(8,128)(2,1)S(1)}, bf16[64,448]{1,0:T(8,128)(2,1)S(1)}, u32[]{:S(2)}, u32[]{:S(2)}) %collective-permute-start.3) | collective-permute-done | bytes 57376 | tf_op jit(solution)/shard_map/ppermute | solution.py:76
  127.1 5.5 %collective-permute-done.4 = bf16[64,448]{1,0:T(8,128)(2,1)S(1)} collective-permute-done((bf16[64,448]{1,0:T(8,128)(2,1)S(1)}, bf16[64,448]{1,0:T(8,128)(2,1)S(1)}, u32[]{:S(2)}, u32[]{:S(2)}) %collective-permute-start.4) | collective-permute-done | bytes 57376 | tf_op jit(solution)/shard_map/ppermute | solution.py:76
  132.6 2.1 reshape_squeeze.6
  134.7 4.0 %reshape_squeeze.7 = bf16[16,128,4,128]{3,2,1,0:T(4,128)(2,1)} reshape(bf16[1,16,128,512]{3,2,1,0:T(8,128)(2,1)} %param.16) | data formatting | bytes 4194304 | tf_op jit(solution)/shard_map/reshape;squeeze | solution.py:132
  138.7 5.5 %collective-permute-done.6 = bf16[64,448]{1,0:T(8,128)(2,1)S(1)} collective-permute-done((bf16[64,448]{1,0:T(8,128)(2,1)S(1)}, bf16[64,448]{1,0:T(8,128)(2,1)S(1)}, u32[]{:S(2)}, u32[]{:S(2)}) %collective-permute-start.6) | collective-permute-done | bytes 57376 | tf_op jit(solution)/shard_map/ppermute | solution.py:76
  148.9 5.6 %bitcast_reduce_fusion = (f32[16,32,4,5]{1,3,2,0:T(8,128)S(1)}, f32[16,4,32,5,128]{4,2,3,1,0:T(8,128)}) fusion(pred[16,128]{1,0:T(8,128)(4,1)S(1)} %add_compare_fusion, bf16[16,128,4,128,1]{3,2,1,0,4:T(4,128)(2,1)} %bitcast.107, bf16[16,32,4,5,128]{4,1,3,2,0:T(8,128)(2,1)S(1)} %gather_fusion, pred[16]{0:T(512)(128)(4,1)S(1)} %compare_and_fusion), kind=kOutput, calls=%fused_computation.13 | convolution fusion | flops 340776960 | bytes 10004496 | tf_op jit(solution)/shard_map/sqkgd,spkd->sqkgp/dot_general | solution.py:113
  155.5 4.2 %fusion.21 = f32[16,32,4,5,128]{4,1,3,2,0:T(8,128)S(1)} fusion(f32[16,4,32,5,128]{4,2,3,1,0:T(8,128)} %get-tuple-element.131, f32[16,32,4,5]{1,3,2,0:T(8,128)S(1)} %copy.169, pred[16,128]{1,0:T(8,128)(4,1)S(1)} %add_compare_fusion, bf16[16,128,4,128,1]{3,2,1,0,4:T(4,128)(2,1)} %bitcast.106), kind=kOutput, calls=%fused_computation.31 | convolution fusion | flops 342097920 | bytes 12625920 | tf_op jit(solution)/shard_map/sqkgp,spkd->sqkgd/dot_general | solution.py:129
  159.8 7.4 %fusion.6 = f32[2,32,4,5,128]{4,0,3,2,1:T(2,128)S(1)} fusion(f32[16,32,4,5,128]{4,1,3,2,0:T(8,128)S(1)} %fusion.21, s32[16,2]{0,1:T(2,128)S(1)} %get-tuple-element.90), kind=kOutput, calls=%fused_computation.16 | convolution fusion | flops 31457312 | bytes 5898368 | tf_op jit(solution)/shard_map/sr,sqkgd->rqkgd/dot_general | solution.py:139
  168.3 2.6 reshape.151
  170.8 4.0 %reshape.153 = bf16[2,2,512,4,128]{4,3,2,1,0:T(4,128)(2,1)} reshape(bf16[2,2,512,512]{3,2,1,0:T(8,128)(2,1)} %param.19) | data formatting | bytes 4194304 | tf_op jit(solution)/shard_map/reshape | solution.py:187
  175.8 6.0 %fusion.9 = f32[16,32,4,5]{1,3,2,0:T(8,128)} fusion(f32[16,4,32,5,128]{4,2,3,1,0:T(8,128)} %get-tuple-element.131, f32[16,32,4,5]{1,3,2,0:T(8,128)S(1)} %copy.169, pred[16,128]{1,0:T(8,128)(4,1)S(1)} %add_compare_fusion), kind=kLoop, calls=%fused_computation.20 | loop fusion | flops 6543360 | bytes 5326848 | tf_op jit(solution)/shard_map/reduce_sum | solution.py:128
  182.9 2.4 fusion.66
  185.3 26.7 %all-gather = f32[16,16,2,4,5]{1,3,4,2,0:T(4,128)S(1)} all-gather(f32[2,16,2,4,5]{1,3,4,2,0:T(4,128)S(1)} %copy.172), channel_id=2, replica_groups=mesh['row'=32,'col'=8] {'col'}, dimensions={0}, use_global_device_ids=true | all-gather | bytes 46080 | tf_op jit(solution)/shard_map/all_gather | solution.py:16
  212.0 1.6 fusion.105
  216.4 26.0 %all_gather.9 = f32[8,2,16,2,4,5]{2,4,5,3,1,0:T(4,128)S(1)} all-gather(f32[1,2,16,2,4,5]{2,4,5,3,1,0:T(4,128)S(1)} %copy.167), channel_id=1, replica_groups=mesh['row'=32,'col'=8] {'col'}, dimensions={0}, use_global_device_ids=true | all-gather | bytes 46080 | tf_op jit(solution)/shard_map/all_gather | solution.py:16
  248.4 5.0 %slice.66 = f32[7,2,16,2,4,5,128]{6,2,5,4,3,1,0:T(8,128)} slice(f32[8,2,16,2,4,5,128]{6,2,5,4,3,1,0:T(8,128)} %all-gather.3.cloned.1.call-done), slice={[1:8], [0:2], [0:16], [0:2], [0:4], [0:5], [0:128]} | slice | bytes 9175040 | tf_op jit(solution)/shard_map/slice | solution.py:18
  253.5 16.7 %while.14 = (s32[]{:T(128)}, f32[2,16,2,4,5]{1,3,4,2,0:T(4,128)S(1)}, f32[2,16,2,4,5]{1,3,4,2,0:T(4,128)S(1)}, f32[2,16,2,4,5,128]{5,4,3,2,1,0:T(8,128)S(1)}, f3...) while((s32[]{:T(128)}, ...), condition=%wide.region_9.10_spmd, body=%wide.region_8.9_spmd.sunk | while | flops 499202 | bytes 3348581 | solution.py:19
  270.6 2.1 fusion.55
  (136 shorter events, 38.8 us)
Async XLA Ops:
  6.5 1.0 copy-start
  6.5 4.6 %copy-start.12 = (s32[2,64]{1,0:T(2,128)S(1)}, s32[2,64]{1,0:T(2,128)}, u32[]{:S(2)}) copy-start(s32[2,64]{1,0:T(2,128)} %param.13) | copy-start | bytes 1540
  6.5 4.9 %copy-start.10 = (s32[2,16]{1,0:T(2,128)S(1)}, s32[2,16]{1,0:T(2,128)}, u32[]{:S(2)}) copy-start(s32[2,16]{1,0:T(2,128)} %param.17) | copy-start | bytes 388
  6.5 4.9 %copy-start.11 = (s32[2]{0:T(128)S(1)}, s32[2]{0:T(128)}, u32[]{:S(2)}) copy-start(s32[2]{0:T(128)} %param.14) | copy-start | bytes 28
  6.5 126.1 %copy-start.5 = (bf16[1,16,128,512]{3,2,1,0:T(8,128)(2,1)S(1)}, bf16[1,16,128,512]{3,2,1,0:T(8,128)(2,1)}, u32[]{:S(2)}) copy-start(bf16[1,16,128,512]{3,2,1,0:T(8,128)(2,1)} %param.15) | copy-start | bytes 6291460
  6.5 96.9 %reduce-scatter.2.cloned.1.call-start = ((), (), s32[]{:S(2)}) async-start(), calls=%async_computation.1 | async-start | bytes 4325376 | tf_op jit(solution)/shard_map/reduce_scatter | solution.py:70
  11.1 235.9 %all-gather.3.cloned.1.call-start = ((), (), s32[]{:S(2)}) async-start(), calls=%async_computation.2 | async-start | bytes 5898240 | tf_op jit(solution)/shard_map/all_gather | solution.py:16
  11.7 134.8 %copy-start.8 = (f32[2,16,2,64]{3,1,2,0:T(8,128)}, f32[2,16,2,64]{3,1,2,0:T(8,128)S(1)}, u32[]{:S(2)}) copy-start(f32[2,16,2,64]{3,1,2,0:T(8,128)S(1)} %get-tuple-element.124) | copy-start | bytes 49156
  11.7 134.8 %copy-start.9 = (f32[2,16,2,64]{3,1,2,0:T(8,128)}, f32[2,16,2,64]{3,1,2,0:T(8,128)S(1)}, u32[]{:S(2)}) copy-start(f32[2,16,2,64]{3,1,2,0:T(8,128)S(1)} %get-tuple-element.125) | copy-start | bytes 49156
  104.4 5.6 %collective-permute-start = (bf16[64,448]{1,0:T(8,128)(2,1)S(1)}, bf16[64,448]{1,0:T(8,128)(2,1)S(1)}, u32[]{:S(2)}, u32[]{:S(2)}) collective-permute-start(bf16[64,448]{1,0:T(8,128)(2,1)S(1)} %convert_element_type.48), channel_id=1, source_target_pairs={{0,1},{1,2},{2,3},{3,4},{4,5},{5,6},{6,7},{7,0},{8,9},{9,10},{10,1... | collective-permute-start | bytes 172040 | tf_op jit(solution)/shard_map/ppermute | solution.py:76
  110.0 6.1 %collective-permute-start.1 = (bf16[64,448]{1,0:T(8,128)(2,1)S(1)}, bf16[64,448]{1,0:T(8,128)(2,1)S(1)}, u32[]{:S(2)}, u32[]{:S(2)}) collective-permute-start(bf16[64,448]{1,0:T(8,128)(2,1)S(1)} %collective-permute-done), channel_id=1, source_target_pairs={{0,1},{1,2},{2,3},{3,4},{4,5},{5,6},{6,7},{7,0},{8,9},{9,10},{10,1... | collective-permute-start | bytes 172040 | tf_op jit(solution)/shard_map/ppermute | solution.py:76
  116.2 5.5 %collective-permute-start.2 = (bf16[64,448]{1,0:T(8,128)(2,1)S(1)}, bf16[64,448]{1,0:T(8,128)(2,1)S(1)}, u32[]{:S(2)}, u32[]{:S(2)}) collective-permute-start(bf16[64,448]{1,0:T(8,128)(2,1)S(1)} %collective-permute-done.1), channel_id=1, source_target_pairs={{0,1},{1,2},{2,3},{3,4},{4,5},{5,6},{6,7},{7,0},{8,9},{9,10},{10,1... | collective-permute-start | bytes 172040 | tf_op jit(solution)/shard_map/ppermute | solution.py:76
  121.6 5.5 %collective-permute-start.3 = (bf16[64,448]{1,0:T(8,128)(2,1)S(1)}, bf16[64,448]{1,0:T(8,128)(2,1)S(1)}, u32[]{:S(2)}, u32[]{:S(2)}) collective-permute-start(bf16[64,448]{1,0:T(8,128)(2,1)S(1)} %collective-permute-done.2), channel_id=1, source_target_pairs={{0,1},{1,2},{2,3},{3,4},{4,5},{5,6},{6,7},{7,0},{8,9},{9,10},{10,1... | collective-permute-start | bytes 172040 | tf_op jit(solution)/shard_map/ppermute | solution.py:76
  127.1 5.5 %collective-permute-start.4 = (bf16[64,448]{1,0:T(8,128)(2,1)S(1)}, bf16[64,448]{1,0:T(8,128)(2,1)S(1)}, u32[]{:S(2)}, u32[]{:S(2)}) collective-permute-start(bf16[64,448]{1,0:T(8,128)(2,1)S(1)} %collective-permute-done.3), channel_id=1, source_target_pairs={{0,1},{1,2},{2,3},{3,4},{4,5},{5,6},{6,7},{7,0},{8,9},{9,10},{10,1... | collective-permute-start | bytes 172040 | tf_op jit(solution)/shard_map/ppermute | solution.py:76
  132.6 6.1 %collective-permute-start.5 = (bf16[64,448]{1,0:T(8,128)(2,1)S(1)}, bf16[64,448]{1,0:T(8,128)(2,1)S(1)}, u32[]{:S(2)}, u32[]{:S(2)}) collective-permute-start(bf16[64,448]{1,0:T(8,128)(2,1)S(1)} %collective-permute-done.4), channel_id=1, source_target_pairs={{0,1},{1,2},{2,3},{3,4},{4,5},{5,6},{6,7},{7,0},{8,9},{9,10},{10,1... | collective-permute-start | bytes 172040 | tf_op jit(solution)/shard_map/ppermute | solution.py:76
  138.7 5.5 %collective-permute-start.6 = (bf16[64,448]{1,0:T(8,128)(2,1)S(1)}, bf16[64,448]{1,0:T(8,128)(2,1)S(1)}, u32[]{:S(2)}, u32[]{:S(2)}) collective-permute-start(bf16[64,448]{1,0:T(8,128)(2,1)S(1)} %collective-permute-done.5), channel_id=1, source_target_pairs={{0,1},{1,2},{2,3},{3,4},{4,5},{5,6},{6,7},{7,0},{8,9},{9,10},{10,1... | collective-permute-start | bytes 172040 | tf_op jit(solution)/shard_map/ppermute | solution.py:76
  145.1 0.8 copy-start.6
  146.8 0.7 copy-start.1
  146.8 0.9 copy-start.3
  175.0 40.2 %copy-start.2 = (bf16[2,16,2,20,64]{4,3,1,2,0:T(8,128)(2,1)S(1)}, bf16[2,16,2,20,64]{4,3,1,2,0:T(8,128)(2,1)}, u32[]{:S(2)}) copy-start(bf16[2,16,2,20,64]{4,3,1,2,0:T(8,128)(2,1)} %copy-done.1) | copy-start | bytes 491524
  175.0 40.2 %copy-start.4 = (bf16[2,16,2,20,64]{4,3,1,2,0:T(8,128)(2,1)S(1)}, bf16[2,16,2,20,64]{4,3,1,2,0:T(8,128)(2,1)}, u32[]{:S(2)}) copy-start(bf16[2,16,2,20,64]{4,3,1,2,0:T(8,128)(2,1)} %copy-done.3) | copy-start | bytes 491524
  242.4 3.6 %copy-start.7 = (f32[8,2,16,2,4,5]{2,4,5,3,1,0:T(4,128)}, f32[8,2,16,2,4,5]{2,4,5,3,1,0:T(4,128)S(1)}, u32[]{:S(2)}) copy-start(f32[8,2,16,2,4,5]{2,4,5,3,1,0:T(4,128)S(1)} %all_gather.9) | copy-start | bytes 122884
  248.4 5.0 %slice-start = ((f32[8,2,16,2,4,5]{2,4,5,3,1,0:T(4,128)}), f32[7,2,16,2,4,5]{2,4,5,3,1,0:T(4,128)S(1)}, s32[]{:S(2)}) async-start(f32[8,2,16,2,4,5]{2,4,5,3,1,0:T(4,128)} %copy-done.7), calls=%async_computation.3 | async-start | bytes 573440 | tf_op jit(solution)/shard_map/slice | solution.py:18
Sparse Core Ops, SparseCore 0:
  11.3 92.0 reduce-scatter.1
  168.4 69.5 all-gather.2
